TPU v7x, 32 devices: a whole 2x2x4 slice. The times are simulated.
32 devices in a mesh: batch: 8 (over z, y), grp: 4 (over x, core).
Axes of the slice: x: 2, y: 2, z: 4, core: 2. Of those that a mesh axis runs over, the one named last changes fastest.
Arguments:
- tokens: bfloat16 [8192, 768], P(('batch', 'grp')), may hold values from -6 to 6
- dest: int32 [8192, 1], P(('batch', 'grp')), may hold values from 0 to 7; in each aligned block of 256 rows (0 to 255, 256 to 511, ...) at most 64 rows name the same one
- seg_ids: int32 [32, 512], P(('batch', 'grp')), may hold values from 0 to 7, never falling along the last dimension, each value on 1 to 128 neighbouring positions
- cot_out: bfloat16 [8192, 768], P(('batch', 'grp')), may hold values from -6 to 6
- cot_align: bfloat16 [8192, 1024], P(('batch', 'grp')), may hold values from -6 to 6
- ln1_gain: bfloat16 [768], replicated, may hold values from 0.5 to 1.5
- ln1_bias: bfloat16 [768], replicated, may hold values from -1 to 1
- w_qkv: bfloat16 [768, 2304], replicated, may hold values from -0.21875 to 0.21875
- q_bias: bfloat16 [768], replicated, may hold values from -1 to 1
- v_bias: bfloat16 [768], replicated, may hold values from -1 to 1
- w_out: bfloat16 [768, 768], replicated, may hold values from -1.75 to 1.75
- out_bias: bfloat16 [768], replicated, may hold values from -1 to 1
- ln2_gain: bfloat16 [768], replicated, may hold values from 0.5 to 1.5
- ln2_bias: bfloat16 [768], replicated, may hold values from -1 to 1
- w_up: bfloat16 [768, 3072], replicated, may hold values from -0.21875 to 0.21875
- up_bias: bfloat16 [3072], replicated, may hold values from -1 to 1
- w_down: bfloat16 [3072, 768], replicated, may hold values from -0.109375 to 0.109375
- down_bias: bfloat16 [768], replicated, may hold values from -1 to 1
- ln3_gain: bfloat16 [768], replicated, may hold values from 0.5 to 1.5
- ln3_bias: bfloat16 [768], replicated, may hold values from -1 to 1
- w_align: bfloat16 [768, 1024], replicated, may hold values from -0.21875 to 0.21875
- align_bias: bfloat16 [1024], replicated, may hold values from -1 to 1
Outputs:
- out_tokens: bfloat16 [8192, 768], P(('batch', 'grp'))
- aligned_tokens: bfloat16 [8192, 1024], P(('batch', 'grp'))
- grad_tokens: bfloat16 [8192, 768], P(('batch', 'grp'))
- grad_ln1_gain: float32 [768], replicated
- grad_ln1_bias: float32 [768], replicated
- grad_w_qkv: float32 [768, 2304], P('batch', 'grp')
- grad_q_bias: float32 [768], replicated
- grad_v_bias: float32 [768], replicated
- grad_w_out: float32 [768, 768], P('batch', 'grp')
- grad_out_bias: float32 [768], replicated
- grad_ln2_gain: float32 [768], replicated
- grad_ln2_bias: float32 [768], replicated
- grad_w_up: float32 [768, 3072], P('batch', 'grp')
- grad_up_bias: float32 [3072], replicated
- grad_w_down: float32 [3072, 768], P('batch', 'grp')
- grad_down_bias: float32 [768], replicated
- grad_ln3_gain: float32 [768], replicated
- grad_ln3_bias: float32 [768], replicated
- grad_w_align: float32 [768, 1024], P('batch', 'grp')
- grad_align_bias: float32 [1024], replicated
Inputs may be any that keep to these rules, and one draw needn't show every extreme that they name: `dest`: within the 256 rows of one device no destination is named by more than 64 rows, a bound that some block reaches. `seg_ids`: along each device's 512 slots the clip numbers never fall; each clip takes 1 to 128 slots and some clip exactly 128.
All inputs are finite; a program needn't handle non-finite values.
Results may differ from a plain program's by a relative error of at most 0.012.
Values may be sent and summed in bfloat16 or wider, within the bound.
No kernel may reach another device: no remote copies, remote signals or barrier semaphores. Data moves between devices by JAX's collectives and lax.ppermute only.
A program may use at most 192 MiB of HBM per device.

v0:
```python
import jax
import jax.numpy as jnp
from jax import lax
from jax.sharding import PartitionSpec as P

H = 12
layer_eps = 1e-06
masked_value = -1e30


def normalize(values, gain_row, shift_row):
    average = jnp.mean(values, axis=-1, keepdims=True)
    centered = values - average
    variance = jnp.mean(centered * centered, axis=-1, keepdims=True)
    return centered * lax.rsqrt(variance + layer_eps) * gain_row + shift_row


def exact_gelu(values):
    return jax.nn.gelu(values, approximate=False)


def row_matmul(left_side, right_side):
    return jnp.dot(left_side, right_side, preferred_element_type=jnp.float32)


def left_transposed(left_side, right_side):
    return lax.dot_general(
        left_side, right_side, (((0,), (0,)), ((), ())), preferred_element_type=jnp.float32
    )


def right_transposed(left_side, right_side):
    return lax.dot_general(
        left_side, right_side, (((1,), (1,)), ((), ())), preferred_element_type=jnp.float32
    )


def column_sum(values):
    return jnp.sum(values.astype(jnp.float32), axis=0)


def tiled_blocks(matrix, row_parts, column_parts):
    rows_total, columns_total = matrix.shape
    shaped = matrix.reshape(
        row_parts, rows_total // row_parts, column_parts, columns_total // column_parts
    )
    shaped = jnp.transpose(shaped, (0, 2, 1, 3))
    return shaped.reshape(
        row_parts * column_parts, rows_total // row_parts, columns_total // column_parts
    )


def per_device(
    tokens,
    dest,
    seg_ids,
    cot_out,
    cot_align,
    ln1_gain,
    ln1_bias,
    w_qkv,
    q_bias,
    v_bias,
    w_out,
    out_bias,
    ln2_gain,
    ln2_bias,
    w_up,
    up_bias,
    w_down,
    down_bias,
    ln3_gain,
    ln3_bias,
    w_align,
    align_bias,
):
    model_width = tokens.shape[1]
    align_width = cot_align.shape[1]
    seq_rows = seg_ids.shape[1]
    peer_count = lax.axis_size("batch")
    group_count = lax.axis_size("grp")
    capacity = seq_rows // peer_count
    head_count = H
    head_size = model_width // head_count
    score_scale = head_size ** (-0.5)
    targets = dest[:, 0]
    onehot = (targets[:, None] == jnp.arange(peer_count, dtype=jnp.int32)[None, :]).astype(
        jnp.int32
    )
    earlier = jnp.cumsum(onehot, axis=0) - onehot
    offset = jnp.sum(earlier * onehot, axis=1)
    slot_index = targets * capacity + offset

    def pack_rows(rows):
        empty = jnp.zeros((seq_rows,) + rows.shape[1:], rows.dtype)
        return empty.at[slot_index].set(rows).reshape((peer_count, capacity) + rows.shape[1:])

    flag_rows = jnp.ones((tokens.shape[0],), jnp.bfloat16)
    recv_rows, recv_grad, recv_align, recv_flag = (
        lax.all_to_all(pack_rows(tokens), "batch", split_axis=0, concat_axis=0, tiled=True),
        lax.all_to_all(pack_rows(cot_out), "batch", split_axis=0, concat_axis=0, tiled=True),
        lax.all_to_all(pack_rows(cot_align), "batch", split_axis=0, concat_axis=0, tiled=True),
        lax.all_to_all(pack_rows(flag_rows), "batch", split_axis=0, concat_axis=0, tiled=True),
    )
    inputs = recv_rows.reshape(seq_rows, model_width).astype(jnp.float32)
    is_live = recv_flag.reshape(seq_rows) > 0.5
    segments = seg_ids[0]
    key_index = jnp.arange(seq_rows, dtype=jnp.int32)
    block_rows = min(512, seq_rows)
    gain_one = ln1_gain.astype(jnp.float32)
    normed_one, norm_one_back = jax.vjp(normalize, inputs, gain_one, ln1_bias.astype(jnp.float32))
    act_one = normed_one.astype(jnp.bfloat16)
    joined = row_matmul(act_one, w_qkv)
    queries = (
        (joined[:, :model_width] + q_bias.astype(jnp.float32))
        .astype(jnp.bfloat16)
        .reshape(seq_rows, head_count, head_size)
    )
    key_rows = (
        joined[:, model_width : 2 * model_width]
        .astype(jnp.bfloat16)
        .reshape(seq_rows, head_count, head_size)
    )
    value_rows = (
        (joined[:, 2 * model_width :] + v_bias.astype(jnp.float32))
        .astype(jnp.bfloat16)
        .reshape(seq_rows, head_count, head_size)
    )

    def block_scores(block_start):
        query_index = block_start + jnp.arange(block_rows, dtype=jnp.int32)
        same_clip = segments[:, None] == segments[None, :]
        usable = is_live[None, :] | (query_index[:, None] == key_index[None, :])
        raw_scores = (
            jnp.einsum("qhd,khd->hqk", queries, key_rows, preferred_element_type=jnp.float32)
            * score_scale
        )
        return jnp.where((same_clip & usable)[None], raw_scores, masked_value)

    block_start = 0
    scores = block_scores(block_start)
    row_max = jnp.max(scores, axis=-1, keepdims=True)
    powered = jnp.exp(scores - row_max)
    denominator = jnp.sum(powered, axis=-1, keepdims=True)
    probs_low = (powered / denominator).astype(jnp.bfloat16)
    context_parts = jnp.einsum(
        "hqk,khd->qhd", probs_low, value_rows, preferred_element_type=jnp.float32
    )
    lse_parts = [row_max + jnp.log(denominator)]
    context = context_parts.reshape(seq_rows, model_width).astype(jnp.bfloat16)
    middle = inputs + row_matmul(context, w_out) + out_bias.astype(jnp.float32)
    normed_two, norm_two_back = jax.vjp(
        normalize, middle, ln2_gain.astype(jnp.float32), ln2_bias.astype(jnp.float32)
    )
    act_two = normed_two.astype(jnp.bfloat16)
    hidden_pre = row_matmul(act_two, w_up) + up_bias.astype(jnp.float32)
    hidden_act, gelu_back = jax.vjp(exact_gelu, hidden_pre)
    hidden_low = hidden_act.astype(jnp.bfloat16)
    result = middle + row_matmul(hidden_low, w_down) + down_bias.astype(jnp.float32)
    normed_three, norm_three_back = jax.vjp(
        normalize, result, ln3_gain.astype(jnp.float32), ln3_bias.astype(jnp.float32)
    )
    act_three = normed_three.astype(jnp.bfloat16)
    aligned = row_matmul(act_three, w_align) + align_bias.astype(jnp.float32)
    grad_aligned = recv_align.reshape(seq_rows, align_width)
    grad_w_align = left_transposed(act_three, grad_aligned)
    grad_align_bias = column_sum(grad_aligned)
    grad_result_part, grad_ln3_gain, grad_ln3_bias = norm_three_back(
        right_transposed(grad_aligned, w_align)
    )
    grad_result = recv_grad.reshape(seq_rows, model_width).astype(jnp.float32) + grad_result_part
    grad_mlp = grad_result.astype(jnp.bfloat16)
    grad_w_down = left_transposed(hidden_low, grad_mlp)
    grad_down_bias = column_sum(grad_mlp)
    (grad_pre,) = gelu_back(right_transposed(grad_mlp, w_down))
    grad_pre_low = grad_pre.astype(jnp.bfloat16)
    grad_w_up = left_transposed(act_two, grad_pre_low)
    grad_up_bias = column_sum(grad_pre_low)
    grad_middle_part, grad_ln2_gain, grad_ln2_bias = norm_two_back(
        right_transposed(grad_pre_low, w_up)
    )
    grad_middle = grad_result + grad_middle_part
    grad_branch = grad_middle.astype(jnp.bfloat16)
    grad_w_out = left_transposed(context, grad_branch)
    grad_out_bias = column_sum(grad_branch)
    grad_context = (
        right_transposed(grad_branch, w_out)
        .astype(jnp.bfloat16)
        .reshape(seq_rows, head_count, head_size)
    )
    grad_keys = jnp.zeros((seq_rows, head_count, head_size), jnp.float32)
    grad_values = jnp.zeros((seq_rows, head_count, head_size), jnp.float32)
    query_parts = []
    for block_number, block_start in enumerate(range(0, seq_rows, block_rows)):
        scores = block_scores(block_start)
        probs = jnp.exp(scores - lse_parts[block_number])
        probs_low = probs.astype(jnp.bfloat16)
        grad_values = jnp.einsum(
            "hqk,qhd->khd", probs_low, grad_context, preferred_element_type=jnp.float32
        )
        grad_probs = jnp.einsum(
            "qhd,khd->hqk", grad_context, value_rows, preferred_element_type=jnp.float32
        )
        inner_sum = jnp.sum(grad_probs * probs, axis=-1, keepdims=True)
        grad_scores = (probs * (grad_probs - inner_sum)).astype(jnp.bfloat16)
        query_parts.append(
            jnp.einsum("hqk,khd->qhd", grad_scores, key_rows, preferred_element_type=jnp.float32)
            * score_scale
        )
        grad_keys = (
            jnp.einsum("hqk,qhd->khd", grad_scores, queries, preferred_element_type=jnp.float32)
            * score_scale
        )
    grad_queries = query_parts[0]
    grad_joined = jnp.concatenate(
        [
            grad_queries.reshape(seq_rows, model_width),
            grad_keys.reshape(seq_rows, model_width),
            grad_values.reshape(seq_rows, model_width),
        ],
        axis=1,
    ).astype(jnp.bfloat16)
    grad_w_qkv = left_transposed(act_one, grad_joined)
    grad_q_bias = column_sum(grad_joined[:, :model_width])
    grad_v_bias = column_sum(grad_joined[:, 2 * model_width :])
    grad_input_part, grad_ln1_gain, grad_ln1_bias = norm_one_back(
        right_transposed(grad_joined, w_qkv)
    )
    grad_input = grad_middle + grad_input_part

    def block_view(rows):
        return rows.reshape((peer_count, capacity) + rows.shape[1:])

    back_result, back_aligned, back_grad = (
        lax.all_to_all(
            block_view(result.astype(jnp.bfloat16)),
            "batch",
            split_axis=0,
            concat_axis=0,
            tiled=True,
        ),
        lax.all_to_all(
            block_view(aligned.astype(jnp.bfloat16)),
            "batch",
            split_axis=0,
            concat_axis=0,
            tiled=True,
        ),
        lax.all_to_all(
            block_view(grad_input.astype(jnp.bfloat16)),
            "batch",
            split_axis=0,
            concat_axis=0,
            tiled=True,
        ),
    )
    out_tokens = back_result.reshape(seq_rows, model_width)[slot_index]
    aligned_tokens = back_aligned.reshape(seq_rows, align_width)[slot_index]
    grad_tokens = back_grad.reshape(seq_rows, model_width)[slot_index]
    (
        sum_ln1_gain,
        sum_ln1_bias,
        sum_q_bias,
        sum_v_bias,
        sum_out_bias,
        sum_ln2_gain,
        sum_ln2_bias,
        sum_up_bias,
        sum_down_bias,
        sum_ln3_gain,
        sum_ln3_bias,
        sum_align_bias,
    ) = lax.psum(
        (
            grad_ln1_gain,
            grad_ln1_bias,
            grad_q_bias,
            grad_v_bias,
            grad_out_bias,
            grad_ln2_gain,
            grad_ln2_bias,
            grad_up_bias,
            grad_down_bias,
            grad_ln3_gain,
            grad_ln3_bias,
            grad_align_bias,
        ),
        ("batch", "grp"),
    )
    block_sums = (
        lax.psum_scatter(
            tiled_blocks(grad_w_qkv, peer_count, group_count),
            ("batch", "grp"),
            scatter_dimension=0,
            tiled=True,
        ),
        lax.psum_scatter(
            tiled_blocks(grad_w_out, peer_count, group_count),
            ("batch", "grp"),
            scatter_dimension=0,
            tiled=True,
        ),
        lax.psum_scatter(
            tiled_blocks(grad_w_up, peer_count, group_count),
            ("batch", "grp"),
            scatter_dimension=0,
            tiled=True,
        ),
        lax.psum_scatter(
            tiled_blocks(grad_w_down, peer_count, group_count),
            ("batch", "grp"),
            scatter_dimension=0,
            tiled=True,
        ),
        lax.psum_scatter(
            tiled_blocks(grad_w_align, peer_count, group_count),
            ("batch", "grp"),
            scatter_dimension=0,
            tiled=True,
        ),
    )
    sum_w_qkv = block_sums[0][0]
    sum_w_out = block_sums[1][0]
    sum_w_up = block_sums[2][0]
    sum_w_down = block_sums[3][0]
    sum_w_align = block_sums[4][0]
    return (
        out_tokens,
        aligned_tokens,
        grad_tokens,
        sum_ln1_gain,
        sum_ln1_bias,
        sum_w_qkv,
        sum_q_bias,
        sum_v_bias,
        sum_w_out,
        sum_out_bias,
        sum_ln2_gain,
        sum_ln2_bias,
        sum_w_up,
        sum_up_bias,
        sum_w_down,
        sum_down_bias,
        sum_ln3_gain,
        sum_ln3_bias,
        sum_w_align,
        sum_align_bias,
    )


def solution(mesh):
    return jax.shard_map(
        per_device,
        mesh=mesh,
        in_specs=(
            P(("batch", "grp"), None),
            P(("batch", "grp"), None),
            P(("batch", "grp"), None),
            P(("batch", "grp"), None),
            P(("batch", "grp"), None),
            P(),
            P(),
            P(),
            P(),
            P(),
            P(),
            P(),
            P(),
            P(),
            P(),
            P(),
            P(),
            P(),
            P(),
            P(),
            P(),
            P(),
        ),
        out_specs=(
            P(("batch", "grp"), None),
            P(("batch", "grp"), None),
            P(("batch", "grp"), None),
            P(),
            P(),
            P("batch", "grp"),
            P(),
            P(),
            P("batch", "grp"),
            P(),
            P(),
            P(),
            P("batch", "grp"),
            P(),
            P("batch", "grp"),
            P(),
            P(),
            P(),
            P("batch", "grp"),
            P(),
        ),
        check_vma=False,
    )
```

profile of v0, /device:TPU:0, one launch (start us, length us, event | category | flops | bytes accessed | tf_op | source)
XLA Modules:
  0.0 800.7 jit_solution(46928050250351384)
XLA Ops:
  11.6 2.2 scatter_custom_fusion.1
  14.4 7.3 all-to-all-start.1
  21.7 3.0 scatter_custom_fusion
  24.7 3.3 all-to-all-done.1
  28.1 4.2 all-to-all-start
  45.7 3.0 scatter_custom_fusion.2
  48.8 3.1 scatter_custom_fusion.3
  54.3 6.3 all-to-all-start.5
  61.9 1.5 fusion.25
  63.5 1.5 fusion.21
  65.1 2.0 fusion.64
  69.5 2.3 copy.90
  71.8 2.3 copy.91
  74.1 2.3 copy.88
  76.5 3.5 fusion.12
  80.0 3.7 fusion
  84.7 4.9 fusion.30
  89.7 2.4 fusion.62
  92.4 20.0 %multiply_convert_fusion.1 = (bf16[512,3072]{1,0:T(8,128)(2,1)S(1)}, f32[512,3072]{1,0:T(8,128)}, f32[512,3072]{1,0:T(8,128)}) fusion(f32[3072]{0:T(1024)S(1)} %copy-done.41, bf16[768,3072]{1,0:T(8,128)(2,1)} %param.36, f32[512,768]{1,0:T(8,128)S(1)} %get-tuple-element.63, f32[768]{0:T(1024)S(1)} %copy-done.50, f32[768]{0:T(1024)S(1)} %copy-done.37, ...), kind=kOutput, calls=%fused_computation.21 | convolution fusion | flops 2521694208 | bytes 22042624 | tf_op jit(solution)/shard_map/dot_general | solution.py:23
  112.5 2.7 fusion.63
  116.6 6.0 all-to-all-start.4
  122.7 4.2 multiply_reduce_fusion.1
  127.0 2.4 fusion.60
  129.4 11.3 %all-to-all-done.4 = bf16[8,64,768]{2,1,0:T(8,128)(2,1)} async-done(((bf16[8,64,768]{2,1,0:T(8,128)(2,1)}), bf16[8,64,768]{2,1,0:T(8,128)(2,1)}, u32[]{:S(2)}, u32[]{:S(2)}) %all-to-all-start.4) | async-done | bytes 786464 | tf_op jit(solution)/shard_map/all_to_all | solution.py:101
  140.7 2.5 convert_reduce_fusion.3
  143.2 9.8 %convert_reduce_fusion = (f32[3072]{0:T(1024)}, bf16[512,3072]{1,0:T(8,128)(2,1)S(1)}) fusion(f32[512,3072]{1,0:T(8,128)} %get-tuple-element.53, f32[512,3072]{1,0:T(8,128)} %get-tuple-element.64, f32[3072]{0:T(1024)S(1)} %copy-done.42, bf16[512,768]{1,0:T(8,128)(2,1)S(1)} %get-tuple-element.45, bf16[3072,768]{1,0:T(8,128)(2,1)} %param.38), kind=kOutput, calls=%fused_computation.18 | convolution fusion | flops 2442654720 | bytes 21258240 | tf_op jit(solution)/shard_map/dot_general | solution.py:33
  153.0 7.0 multiply_reduce_fusion.2
  161.5 3.0 convert_bitcast_fusion
  164.5 2.3 copy.98
  166.8 4.0 fusion.66
  170.9 2.3 copy.97
  174.6 2.4 copy.103
  177.0 2.3 copy.102
  179.3 3.5 convolution_convert_fusion
  182.8 2.3 copy.93
  185.1 4.1 fusion.68
  189.6 13.7 %multiply_reduce_fusion = (f32[12,512]{1,0:T(8,128)S(1)}, f32[12,512,512]{1,2,0:T(8,128)}) fusion(f32[12,512]{1,0:T(8,128)} %log_add_fusion, f32[12,512,512]{1,2,0:T(8,128)} %copy-done.1, pred[512,512]{0,1:T(8,128)(4,1)} %fusion.32, bf16[512,12,64]{0,2,1:T(8,128)(2,1)} %bitcast.196, bf16[512,12,64]{0,2,1:T(8,128)(2,1)} %bitcast.195), kind=kOutput, calls=%fused_computation.8 | convolution fusion | flops 418375680 | bytes 27049984 | tf_op jit(solution)/shard_map/qhd,khd->hqk/dot_general | solution.py:201
  203.4 7.2 multiply_convert_fusion
  211.8 2.9 multiply_convert_fusion.2
  214.7 3.1 fusion.27
  219.3 4.4 fusion.65
  224.4 8.9 %fusion.53 = f32[768,3072]{1,0:T(8,128)} fusion(bf16[512,3072]{1,0:T(8,128)(2,1)} %copy-done.55, f32[512,768]{1,0:T(8,128)} %copy-done.9, f32[768]{0:T(1024)} %convert_element_type.155, f32[768]{0:T(1024)S(1)} %copy-done.39, f32[512]{0:T(512)S(1)} %copy-done.48, f32[512]{0:T(512)S(1)} %broadcast_multiply_fusion.2), kind=kOutput, calls=%fused_computation.129 | convolution fusion | flops 2417885184 | bytes 14166016 | tf_op jit(solution)/shard_map/dot_general | solution.py:27
  233.2 12.5 %reshape.372 = f32[8,96,4,768]{3,2,1,0:T(4,128)} reshape(f32[768,3072]{1,0:T(8,128)} %fusion.53) | data formatting | bytes 18874368 | tf_op jit(solution)/shard_map/reshape | solution.py:44
  245.8 9.0 %copy.99 = f32[8,4,96,768]{3,2,1,0:T(8,128)} copy(f32[8,4,96,768]{3,1,2,0:T(4,128)} %bitcast.179) | data formatting | bytes 18874368 | tf_op jit(solution)/shard_map/transpose | solution.py:47
  255.3 8.4 %fusion.67 = f32[3072,768]{0,1:T(8,128)} fusion(bf16[512,3072]{1,0:T(8,128)(2,1)} %copy-done.54, bf16[512,768]{1,0:T(8,128)(2,1)} %copy-done.18), kind=kOutput, calls=%fused_computation.141 | convolution fusion | flops 2415919104 | bytes 13369344 | tf_op jit(solution)/shard_map/dot_general | solution.py:27
  263.7 5.9 copy.112
  269.6 5.4 copy.101
  275.7 3.0 add_convert_fusion.1
  278.7 28.1 %all_to_all.40 = bf16[8,64,1024]{2,1,0:T(8,128)(2,1)} all-to-all(bf16[8,64,1024]{2,1,0:T(8,128)(2,1)S(1)} %bitcast.210), channel_id=1, replica_groups=mesh['batch'=8,'grp'=4] {'batch'}, dimensions={0} | all-to-all | bytes 2097152 | tf_op jit(solution)/shard_map/all_to_all | solution.py:242
  306.8 4.2 all-to-all-start.2
  311.1 4.8 fusion.57
  315.9 2.1 fusion.22
  318.0 2.6 convert_reduce_fusion.4
  320.5 12.9 %all-to-all-done.2 = bf16[8,64,768]{2,1,0:T(8,128)(2,1)} async-done(((bf16[8,64,768]{2,1,0:T(8,128)(2,1)}), bf16[8,64,768]{2,1,0:T(8,128)(2,1)}, u32[]{:S(2)}, u32[]{:S(2)}) %all-to-all-start.2) | async-done | bytes 786464 | tf_op jit(solution)/shard_map/all_to_all | solution.py:235
  333.4 4.4 all-to-all-start.6
  339.1 1.4 convert_reduce_fusion.1
  340.5 2.3 convert_reduce_fusion.5
  342.7 43.1 %all-reduce = (f32[768]{0:T(1024)}, f32[768]{0:T(1024)}, f32[768]{0:T(1024)}, f32[768]{0:T(1024)}, f32[768]{0:T(1024)}, /*index=5*/f32[768]{0:T(1024)}, f32[768]...) all-reduce(f32[768]{0:T(1024)S(1)} %get-tuple-element.24, ...), channel_id=1, replica_groups=mesh['batch'=8,'grp'=4] {'batch','grp'}, use_global_device_ids=true, to_apply=%region_23.24 | all-reduce | flops 11776 | bytes 94208 | tf_op jit(solution)/shard_map/psum | solution.py:273
  385.8 3.9 gather_fusion.1
  389.7 3.4 gather_fusion
  393.1 3.4 gather_fusion.2
  396.5 114.2 %reduce-scatter.6.cloned.1.call-done = f32[1,96,576]{2,1,0:T(8,128)} async-done(((f32[32,96,576]{2,1,0:T(8,128)}), f32[1,96,576]{2,1,0:T(8,128)}) %reduce-scatter.6.cloned.1.call-update) | async-done | bytes 221200 | tf_op jit(solution)/shard_map/reduce_scatter | solution.py:291
  510.7 142.3 %reduce-scatter.10.cloned.1.call-done = f32[1,96,768]{2,1,0:T(8,128)} async-done(((f32[32,96,768]{2,1,0:T(8,128)}), f32[1,96,768]{2,1,0:T(8,128)}) %reduce-scatter.10.cloned.1.call-update) | async-done | bytes 294928 | tf_op jit(solution)/shard_map/reduce_scatter | solution.py:303
  653.0 141.0 %reduce-scatter.12.cloned.1.call-done = f32[1,384,192]{1,2,0:T(8,128)} async-done(((f32[32,384,192]{1,2,0:T(8,128)}), f32[1,384,192]{1,2,0:T(8,128)}) %reduce-scatter.12.cloned.1.call-update) | async-done | bytes 294928 | tf_op jit(solution)/shard_map/reduce_scatter | solution.py:309
  (188 shorter events, 36.5 us)
Async XLA Ops:
  7.2 57.8 %copy-start = (bf16[768,2304]{1,0:T(8,128)(2,1)S(1)}, bf16[768,2304]{1,0:T(8,128)(2,1)}, u32[]{:S(2)}) copy-start(bf16[768,2304]{1,0:T(8,128)(2,1)} %param.29) | copy-start | bytes 10616836
  8.6 44.7 %copy-start.43 = (s32[1,512]{1,0:T(1,128)S(1)}, s32[1,512]{1,0:T(1,128)}, u32[]{:S(2)}) copy-start(s32[1,512]{1,0:T(1,128)} %param.24) | copy-start | bytes 6148
  11.6 42.7 %copy-start.49 = (s32[256,1]{0,1:T(1,128)}, s32[256,1]{0,1:T(1,128)S(1)}, u32[]{:S(2)}) copy-start(s32[256,1]{0,1:T(1,128)S(1)} %compare_select_fusion) | copy-start | bytes 3076
  14.4 13.7 %all-to-all-start.1 = ((bf16[8,1,64]{2,1,0:T(2,128)(2,1)}), bf16[8,1,64]{2,1,0:T(2,128)(2,1)S(1)}, u32[]{:S(2)}, u32[]{:S(2)}) async-start(bf16[8,1,64]{2,1,0:T(2,128)(2,1)} %all_to_all.32), calls=%async_computation.1 | async-start | bytes 8192 | tf_op jit(solution)/shard_map/all_to_all | solution.py:103
  28.1 26.2 %all-to-all-start = ((bf16[8,64,768]{2,1,0:T(8,128)(2,1)}), bf16[8,64,768]{2,1,0:T(8,128)(2,1)}, u32[]{:S(2)}, u32[]{:S(2)}) async-start(bf16[8,64,768]{2,1,0:T(8,128)(2,1)} %bitcast.206), calls=%async_computation | async-start | bytes 1572864 | tf_op jit(solution)/shard_map/all_to_all | solution.py:100
  33.0 32.0 %copy-start.22 = (f32[768]{0:T(1024)}, f32[768]{0:T(1024)S(1)}, u32[]{:S(2)}) copy-start(f32[768]{0:T(1024)S(1)} %convert_element_type.142) | copy-start | bytes 9220
  54.3 62.3 %all-to-all-start.5 = ((bf16[8,64,1024]{2,1,0:T(8,128)(2,1)}), bf16[8,64,1024]{2,1,0:T(8,128)(2,1)}, u32[]{:S(2)}, u32[]{:S(2)}) async-start(bf16[8,64,1024]{2,1,0:T(8,128)(2,1)} %bitcast.193), calls=%async_computation.5 | async-start | bytes 2097152 | tf_op jit(solution)/shard_map/all_to_all | solution.py:102
  61.9 5.2 copy-start.24
  63.5 3.6 copy-start.28
  63.5 3.6 copy-start.26
  65.0 2.1 copy-start.14
  65.0 3.1 copy-start.35
  65.0 3.0 copy-start.36
  80.0 4.6 copy-start.1
  80.0 4.7 copy-start.19
  83.7 5.9 copy-start.21
  84.7 4.9 copy-start.52
  84.7 4.9 copy-start.53
  89.6 2.8 copy-start.16
  89.6 2.7 copy-start.37
  89.6 2.7 copy-start.41
  89.7 2.7 copy-start.50
  89.7 22.7 %slice-start.3 = ((s8[4718592]{0:T(1024)(128)(4,1)}), s8[4194304]{0:T(1024)(128)(4,1)S(1)}, s32[]{:S(2)}) async-start(s8[4718592]{0:T(1024)(128)(4,1)} %bitcast.223), calls=%async_computation.20 | async-start | bytes 8388608
  92.0 20.4 %copy-start.9 = (f32[512,768]{1,0:T(8,128)}, f32[512,768]{1,0:T(8,128)S(1)}, u32[]{:S(2)}) copy-start(f32[512,768]{1,0:T(8,128)S(1)} %get-tuple-element.63) | copy-start | bytes 4718596
  92.4 20.0 %copy-start.46 = (f32[512]{0:T(512)}, f32[512]{0:T(512)S(1)}, u32[]{:S(2)}) copy-start(f32[512]{0:T(512)S(1)} %fusion.43) | copy-start | bytes 6148
  92.4 20.0 %copy-start.51 = (f32[768]{0:T(1024)S(1)}, f32[768]{0:T(1024)}, u32[]{:S(2)}) copy-start(f32[768]{0:T(1024)} %convert_element_type.159) | copy-start | bytes 9220
  92.4 20.0 %slice-start.4 = ((s8[4718592]{0:T(1024)(128)(4,1)}), s8[524288]{0:T(1024)(128)(4,1)S(1)}, s32[]{:S(2)}) async-start(s8[4718592]{0:T(1024)(128)(4,1)} %bitcast.223), calls=%async_computation.21 | async-start | bytes 1048576
  112.4 2.7 copy-start.54
  116.6 24.1 %all-to-all-start.4 = ((bf16[8,64,768]{2,1,0:T(8,128)(2,1)}), bf16[8,64,768]{2,1,0:T(8,128)(2,1)}, u32[]{:S(2)}, u32[]{:S(2)}) async-start(bf16[8,64,768]{2,1,0:T(8,128)(2,1)} %bitcast.205), calls=%async_computation.4 | async-start | bytes 1572864 | tf_op jit(solution)/shard_map/all_to_all | solution.py:101
  122.6 273.9 %reduce-scatter.8.cloned.1.call-start = ((), (), s32[]{:S(2)}) async-start(), calls=%async_computation.13 | async-start | bytes 3244032 | tf_op jit(solution)/shard_map/reduce_scatter | solution.py:297
  122.7 4.3 copy-start.44
  122.7 4.3 copy-start.8
  122.7 4.3 copy-start.31
  122.7 4.3 copy-start.33
  140.7 2.5 copy-start.42
  143.2 9.8 %copy-start.18 = (bf16[512,768]{1,0:T(8,128)(2,1)}, bf16[512,768]{1,0:T(8,128)(2,1)S(1)}, u32[]{:S(2)}) copy-start(bf16[512,768]{1,0:T(8,128)(2,1)S(1)} %get-tuple-element.45) | copy-start | bytes 2359300
  143.2 9.8 %copy-start.10 = (f32[512,768]{1,0:T(8,128)S(1)}, f32[512,768]{1,0:T(8,128)}, u32[]{:S(2)}) copy-start(f32[512,768]{1,0:T(8,128)} %copy-done.9) | copy-start | bytes 4718596
  143.2 9.8 %copy-start.38 = (f32[768]{0:T(1024)S(1)}, f32[768]{0:T(1024)}, u32[]{:S(2)}) copy-start(f32[768]{0:T(1024)} %convert_element_type.154) | copy-start | bytes 9220
  143.2 9.8 %copy-start.47 = (f32[512]{0:T(512)S(1)}, f32[512]{0:T(512)}, u32[]{:S(2)}) copy-start(f32[512]{0:T(512)} %copy-done.46) | copy-start | bytes 6148
  153.0 7.1 copy-start.55
  170.8 225.7 %reduce-scatter.14.cloned.1.call-start = ((), (), s32[]{:S(2)}) async-start(), calls=%async_computation.16 | async-start | bytes 3244032 | tf_op jit(solution)/shard_map/reduce_scatter | solution.py:315
  189.3 321.5 %reduce-scatter.6.cloned.1.call-start = ((), (), s32[]{:S(2)}) async-start(), calls=%async_computation.12 | async-start | bytes 8110080 | tf_op jit(solution)/shard_map/reduce_scatter | solution.py:291
  189.5 13.8 %slice-start = ((s8[12582912]{0:T(1024)(128)(4,1)}), s8[4194304]{0:T(1024)(128)(4,1)S(1)}, s32[]{:S(2)}) async-start(s8[12582912]{0:T(1024)(128)(4,1)} %bitcast.175), calls=%async_computation.17 | async-start | bytes 8388608
  189.5 13.8 %slice-start.1 = ((s8[12582912]{0:T(1024)(128)(4,1)}), s8[4194304]{0:T(1024)(128)(4,1)S(1)}, s32[]{:S(2)}) async-start(s8[12582912]{0:T(1024)(128)(4,1)} %bitcast.175), calls=%async_computation.18 | async-start | bytes 8388608
  189.5 13.8 %slice-start.2 = ((s8[12582912]{0:T(1024)(128)(4,1)}), s8[4194304]{0:T(1024)(128)(4,1)S(1)}, s32[]{:S(2)}) async-start(s8[12582912]{0:T(1024)(128)(4,1)} %bitcast.175), calls=%async_computation.19 | async-start | bytes 8388608
  189.5 13.8 %copy-start.6 = (pred[512,512]{0,1:T(8,128)(4,1)S(1)}, pred[512,512]{0,1:T(8,128)(4,1)}, u32[]{:S(2)}) copy-start(pred[512,512]{0,1:T(8,128)(4,1)} %fusion.32) | copy-start | bytes 786436
  189.6 13.8 %copy-start.20 = (f32[12,512]{1,0:T(8,128)S(1)}, f32[12,512]{1,0:T(8,128)}, u32[]{:S(2)}) copy-start(f32[12,512]{1,0:T(8,128)} %log_add_fusion) | copy-start | bytes 73732
  203.4 7.2 copy-start.3
  211.7 6.1 copy-start.4
  211.7 2.9 copy-start.12
  214.7 3.2 copy-start.15
  217.8 5.9 copy-start.13
  217.8 1.5 copy-start.17
  223.7 429.3 %reduce-scatter.10.cloned.1.call-start = ((), (), s32[]{:S(2)}) async-start(), calls=%async_computation.14 | async-start | bytes 9732096 | tf_op jit(solution)/shard_map/reduce_scatter | solution.py:303
  254.8 539.1 %reduce-scatter.12.cloned.1.call-start = ((), (), s32[]{:S(2)}) async-start(), calls=%async_computation.15 | async-start | bytes 9732096 | tf_op jit(solution)/shard_map/reduce_scatter | solution.py:309
  278.6 32.4 %copy-start.23 = (f32[768]{0:T(1024)S(1)}, f32[768]{0:T(1024)}, u32[]{:S(2)}) copy-start(f32[768]{0:T(1024)} %copy-done.22) | copy-start | bytes 9220
  278.6 32.4 %copy-start.25 = (f32[512]{0:T(512)S(1)}, f32[512]{0:T(512)}, u32[]{:S(2)}) copy-start(f32[512]{0:T(512)} %copy-done.24) | copy-start | bytes 6148
  306.8 26.6 %all-to-all-start.2 = ((bf16[8,64,768]{2,1,0:T(8,128)(2,1)}), bf16[8,64,768]{2,1,0:T(8,128)(2,1)}, u32[]{:S(2)}, u32[]{:S(2)}) async-start(bf16[8,64,768]{2,1,0:T(8,128)(2,1)} %bitcast.198), calls=%async_computation.2 | async-start | bytes 1572864 | tf_op jit(solution)/shard_map/all_to_all | solution.py:235
  311.0 4.8 copy-start.29
  311.0 4.8 copy-start.27
  315.9 2.1 copy-start.11
  320.5 22.2 %copy-start.30 = (f32[768]{0:T(1024)S(1)}, f32[768]{0:T(1024)}, u32[]{:S(2)}) copy-start(f32[768]{0:T(1024)} %get-tuple-element.44) | copy-start | bytes 9220
  333.4 59.7 %all-to-all-start.6 = ((bf16[8,64,768]{2,1,0:T(8,128)(2,1)}), bf16[8,64,768]{2,1,0:T(8,128)(2,1)}, u32[]{:S(2)}, u32[]{:S(2)}) async-start(bf16[8,64,768]{2,1,0:T(8,128)(2,1)} %bitcast.201), calls=%async_computation.6 | async-start | bytes 1572864 | tf_op jit(solution)/shard_map/all_to_all | solution.py:249
  385.8 3.9 copy-start.40
  (8 other events, 7.3 us)
Sparse Core Ops, SparseCore 0:
  171.0 100.4 reduce-scatter.7
  277.5 105.4 reduce-scatter.13
  389.2 121.4 reduce-scatter.5
  518.0 134.8 reduce-scatter.9
  659.3 134.6 reduce-scatter.11
where the time goes:
time: 809 us; the launch traced here: 801 us
  waiting for transfers between devices  425 us (53%)
  matrix products  118 us (15%)
  local copies, waits for them, and re-layouts  81.8 us (10%)
  blocking collectives  71.2 us (9%)
  other arithmetic  56.2 us (7%)
  starting transfers between devices  33.2 us (4%)
  between operations  14.8 us (2%)
    reduce_scatter x1, waiting for transfers between devices, per_device(): lax.psum_scatter(tiled_blocks(grad_w_up, peer_count, group_count), ('batc...  142 us
    reduce_scatter x1, waiting for transfers between devices, per_device(): lax.psum_scatter(tiled_blocks(grad_w_down, peer_count, group_count), ('ba...  141 us
    reduce_scatter x1, waiting for transfers between devices, per_device(): lax.psum_scatter(tiled_blocks(grad_w_qkv, peer_count, group_count), ('bat...  114 us
    psum x1, blocking collectives, per_device(): lax.psum((grad_ln1_gain, grad_ln1_bias, grad_q_bias, grad_v_bias, grad_ou...  43.1 us
    dot_general x5, matrix products, row_matmul(): return jnp.dot(left_side, right_side, preferred_element_type=jnp.float32)  30 us
    dot_general x5, matrix products, left_transposed(): lax.dot_general(left_side, right_side, (((0,), (0,)), ((), ())), preferre...  29.8 us
    dot_general x5, matrix products, right_transposed(): lax.dot_general(left_side, right_side, (((1,), (1,)), ((), ())), preferre...  29.4 us
    all_to_all x1, blocking collectives, per_device(): lax.all_to_all(block_view(aligned.astype(jnp.bfloat16)), 'batch', split_a...  28.1 us
  transfers between devices with their start and end apart: 11, of which 6 were waited for; matrix products, arithmetic and copies ran while one was open for 27% of the time, Pallas kernels for 0%

commit v1 on v0

--- a/solution.py
+++ b/solution.py
@@ -6,6 +6,18 @@
 H = 12
 layer_eps = 1e-06
 masked_value = -1e30
+
+
+def keep_up_scales(local_values, dim_at, vals):
+    kept_arr, wide_out = (local_values.shape[:dim_at], local_values.shape[dim_at + 1 :])
+    moved = local_values.reshape(*kept_arr, vals, -1, *wide_out)
+    return jnp.moveaxis(moved, dim_at, 0)
+
+
+def _scan_sheets(x_local, ndim_at):
+    res = list(x_local.shape[1:])
+    res[ndim_at] *= x_local.shape[0]
+    return jnp.moveaxis(x_local, 0, ndim_at).reshape(res)
 
 
 def normalize(values, gain_row, shift_row):
@@ -96,9 +108,24 @@
         return empty.at[slot_index].set(rows).reshape((peer_count, capacity) + rows.shape[1:])
 
     flag_rows = jnp.ones((tokens.shape[0],), jnp.bfloat16)
+
+    def windows_view(raw, axis_tag, x_in, slab_in):
+        even = jax.lax.axis_size(axis_tag)
+        parts_out, known = (even, jax.lax.axis_index(axis_tag))
+        later = keep_up_scales(raw, x_in, parts_out)
+        o_now = later
+        for ix in range(1, parts_out):
+            z1, y = ((known + ix) % parts_out, (known - ix) % parts_out)
+            block_next = lax.dynamic_index_in_dim(later, z1, 0)
+            n_now = map(lambda tick: (tick, (tick + ix) % parts_out), range(parts_out))
+            right_arr = list(n_now)
+            part_next = jax.lax.ppermute(block_next, axis_tag, right_arr)
+            o_now = lax.dynamic_update_slice_in_dim(o_now, part_next, y, axis=0)
+        return _scan_sheets(o_now, slab_in)
+
     recv_rows, recv_grad, recv_align, recv_flag = (
         lax.all_to_all(pack_rows(tokens), "batch", split_axis=0, concat_axis=0, tiled=True),
-        lax.all_to_all(pack_rows(cot_out), "batch", split_axis=0, concat_axis=0, tiled=True),
+        windows_view(pack_rows(cot_out), "batch", 0, 0),
         lax.all_to_all(pack_rows(cot_align), "batch", split_axis=0, concat_axis=0, tiled=True),
         lax.all_to_all(pack_rows(flag_rows), "batch", split_axis=0, concat_axis=0, tiled=True),
     )

time: 809 us -> 813 us (level)
    all_to_all x1 -> x0, waiting for transfers between devices: 11.3 us -> none  [per_device(): lax.all_to_all(pack_rows(cot_out), 'batch', split_axis=0, concat_axis=0,...]
    ppermute x0 -> x7, starting transfers between devices: none -> 10.7 us  [windows_view(): part_next = jax.lax.ppermute(block_next, axis_tag, right_arr)]
    ppermute x0 -> x7, waiting for transfers between devices: none -> 9.16 us  [windows_view(): part_next = jax.lax.ppermute(block_next, axis_tag, right_arr)]
  transfers between devices with their start and end apart: 11 -> 17, of which waited for: 6 -> 6; matrix products, arithmetic and copies ran while one was open for 27% -> 27% of each run, Pallas kernels for 0% -> 0%
where the time goes in v1:
time: 813 us; the launch traced here: 804 us
  waiting for transfers between devices  419 us (52%)
  matrix products  117 us (14%)
  local copies, waits for them, and re-layouts  88.2 us (11%)
  blocking collectives  76.1 us (9%)
  other arithmetic  53.1 us (7%)
  starting transfers between devices  36.2 us (4%)
  between operations  14.9 us (2%)
    reduce_scatter x1, waiting for transfers between devices, per_device(): lax.psum_scatter(tiled_blocks(grad_w_up, peer_count, group_count), ('batc...  142 us
    reduce_scatter x1, waiting for transfers between devices, per_device(): lax.psum_scatter(tiled_blocks(grad_w_down, peer_count, group_count), ('ba...  141 us
    reduce_scatter x1, waiting for transfers between devices, per_device(): lax.psum_scatter(tiled_blocks(grad_w_qkv, peer_count, group_count), ('bat...  110 us
    psum x1, blocking collectives, per_device(): lax.psum((grad_ln1_gain, grad_ln1_bias, grad_q_bias, grad_v_bias, grad_ou...  44.7 us
    all_to_all x1, blocking collectives, per_device(): lax.all_to_all(block_view(aligned.astype(jnp.bfloat16)), 'batch', split_a...  31.4 us
    dot_general x5, matrix products, left_transposed(): lax.dot_general(left_side, right_side, (((0,), (0,)), ((), ())), preferre...  29.9 us
    dot_general x5, matrix products, row_matmul(): return jnp.dot(left_side, right_side, preferred_element_type=jnp.float32)  29.7 us
    dot_general x5, matrix products, right_transposed(): lax.dot_general(left_side, right_side, (((1,), (1,)), ((), ())), preferre...  27.7 us
  transfers between devices with their start and end apart: 17, of which 6 were waited for; matrix products, arithmetic and copies ran while one was open for 27% of the time, Pallas kernels for 0%

profile of v1, /device:TPU:0, one launch (start us, length us, event | category | flops | bytes accessed | tf_op | source)
XLA Modules:
  0.0 804.2 jit_solution(8827934272651982813)
XLA Ops:
  10.3 2.2 scatter_custom_fusion.1
  13.2 7.3 all-to-all-start.1
  20.5 3.1 scatter_custom_fusion
  23.5 3.3 all-to-all-done.1
  26.8 4.2 all-to-all-start
  31.1 3.0 scatter_custom_fusion.2
  34.1 1.5 constant_dynamic-slice_fusion.6
  35.7 1.9 collective-permute-start
  51.0 3.1 scatter_custom_fusion.3
  55.5 1.9 constant_dynamic-slice_fusion
  59.8 3.2 collective-permute-start.6
  64.2 2.3 collective-permute-start.3
  67.8 9.1 %collective-permute-done.2 = bf16[1,1,64,768]{3,2,0,1:T(8,128)(2,1)S(1)} collective-permute-done((bf16[1,1,64,768]{3,2,0,1:T(8,128)(2,1)S(1)}, bf16[1,1,64,768]{3,2,0,1:T(8,128)(2,1)S(1)}, u32[]{:S(2)}, u32[]{:S(2)}) %collective-permute-start.2) | collective-permute-done | bytes 98336 | tf_op jit(solution)/shard_map/ppermute | solution.py:122
  80.2 4.3 all-to-all-start.4
  89.4 2.0 fusion.64
  93.9 2.3 copy.90
  96.2 2.3 copy.91
  98.5 2.3 copy.88
  100.9 3.5 fusion.12
  104.4 3.7 fusion
  109.1 5.3 fusion.30
  114.5 2.4 fusion.62
  117.3 19.6 %multiply_convert_fusion.1 = (bf16[512,3072]{1,0:T(8,128)(2,1)S(1)}, f32[512,3072]{1,0:T(8,128)}, f32[512,3072]{1,0:T(8,128)}) fusion(f32[3072]{0:T(1024)S(1)} %copy-done.41, bf16[768,3072]{1,0:T(8,128)(2,1)} %param.36, f32[512,768]{1,0:T(8,128)S(1)} %get-tuple-element.70, f32[768]{0:T(1024)S(1)} %copy-done.48, f32[768]{0:T(1024)S(1)} %copy-done.37, ...), kind=kOutput, calls=%fused_computation.21 | convolution fusion | flops 2521694208 | bytes 22042624 | tf_op jit(solution)/shard_map/dot_general | solution.py:35
  136.9 2.7 fusion.63
  141.7 4.3 multiply_reduce_fusion.1
  146.1 2.0 fusion.60
  149.0 9.7 %convert_reduce_fusion = (f32[3072]{0:T(1024)}, bf16[512,3072]{1,0:T(8,128)(2,1)}) fusion(f32[512,3072]{1,0:T(8,128)} %get-tuple-element.53, f32[512,3072]{1,0:T(8,128)} %get-tuple-element.71, f32[3072]{0:T(1024)S(1)} %copy-done.42, bf16[512,768]{1,0:T(8,128)(2,1)S(1)} %get-tuple-element.45, bf16[3072,768]{1,0:T(8,128)(2,1)S(1)} %bitcast.227), kind=kOutput, calls=%fused_computation.18 | convolution fusion | flops 2442654720 | bytes 21258240 | tf_op jit(solution)/shard_map/dot_general | solution.py:45
  158.7 5.5 multiply_reduce_fusion.2
  164.9 1.8 convert_bitcast_fusion
  166.7 2.3 copy.98
  169.0 4.1 fusion.66
  173.1 2.3 copy.97
  176.8 2.3 copy.103
  179.1 2.3 copy.102
  181.5 3.5 convolution_convert_fusion
  185.0 2.3 copy.93
  187.3 4.1 fusion.68
  191.8 13.7 %multiply_reduce_fusion = (f32[12,512]{1,0:T(8,128)S(1)}, f32[12,512,512]{1,2,0:T(8,128)}) fusion(f32[12,512]{1,0:T(8,128)} %log_add_fusion, f32[12,512,512]{1,2,0:T(8,128)} %copy-done.1, pred[512,512]{0,1:T(8,128)(4,1)} %fusion.32, bf16[512,12,64]{0,2,1:T(8,128)(2,1)} %bitcast.198, bf16[512,12,64]{0,2,1:T(8,128)(2,1)} %bitcast.197), kind=kOutput, calls=%fused_computation.8 | convolution fusion | flops 418375680 | bytes 27049984 | tf_op jit(solution)/shard_map/qhd,khd->hqk/dot_general | solution.py:228
  205.6 7.2 multiply_convert_fusion
  214.0 2.9 multiply_convert_fusion.2
  216.9 3.1 fusion.27
  221.5 4.4 fusion.65
  226.5 8.9 %fusion.53 = f32[768,3072]{1,0:T(8,128)} fusion(bf16[512,3072]{1,0:T(8,128)(2,1)} %get-tuple-element.47, f32[512,768]{1,0:T(8,128)} %copy-done.9, f32[768]{0:T(1024)} %convert_element_type.155, f32[768]{0:T(1024)S(1)} %copy-done.39, f32[512]{0:T(512)} %copy-done.45, f32[512]{0:T(512)S(1)} %broadcast_multiply_fusion.2), kind=kOutput, calls=%fused_computation.143 | convolution fusion | flops 2417885184 | bytes 14166016 | tf_op jit(solution)/shard_map/dot_general | solution.py:39
  235.4 12.5 %reshape.367 = f32[8,96,4,768]{3,2,1,0:T(4,128)} reshape(f32[768,3072]{1,0:T(8,128)} %fusion.53) | data formatting | bytes 18874368 | tf_op jit(solution)/shard_map/reshape | solution.py:56
  247.9 9.0 %copy.99 = f32[8,4,96,768]{3,2,1,0:T(8,128)} copy(f32[8,4,96,768]{3,1,2,0:T(4,128)} %bitcast.179) | data formatting | bytes 18874368 | tf_op jit(solution)/shard_map/transpose | solution.py:59
  257.4 8.4 %fusion.67 = f32[3072,768]{0,1:T(8,128)} fusion(bf16[512,3072]{1,0:T(8,128)(2,1)} %copy-done.52, bf16[512,768]{1,0:T(8,128)(2,1)} %copy-done.18), kind=kOutput, calls=%fused_computation.155 | convolution fusion | flops 2415919104 | bytes 13369344 | tf_op jit(solution)/shard_map/dot_general | solution.py:39
  265.8 5.9 copy.112
  271.7 5.3 copy.101
  277.8 3.0 add_convert_fusion.1
  280.8 31.4 %all_to_all.35 = bf16[8,64,1024]{2,1,0:T(8,128)(2,1)} all-to-all(bf16[8,64,1024]{2,1,0:T(8,128)(2,1)S(1)} %bitcast.211), channel_id=1, replica_groups=mesh['batch'=8,'grp'=4] {'batch'}, dimensions={0} | all-to-all | bytes 2097152 | tf_op jit(solution)/shard_map/all_to_all | solution.py:269
  312.2 4.2 all-to-all-start.2
  316.5 4.8 fusion.57
  321.3 2.1 fusion.22
  323.4 3.2 convert_reduce_fusion.4
  326.6 13.0 %all-to-all-done.2 = bf16[8,64,768]{2,1,0:T(8,128)(2,1)} async-done(((bf16[8,64,768]{2,1,0:T(8,128)(2,1)}), bf16[8,64,768]{2,1,0:T(8,128)(2,1)}, u32[]{:S(2)}, u32[]{:S(2)}) %all-to-all-start.2) | async-done | bytes 786464 | tf_op jit(solution)/shard_map/all_to_all | solution.py:262
  339.6 4.4 all-to-all-start.5
  346.7 2.3 convert_reduce_fusion.5
  349.0 44.7 %all-reduce = (f32[768]{0:T(1024)}, f32[768]{0:T(1024)}, f32[768]{0:T(1024)}, f32[768]{0:T(1024)}, f32[768]{0:T(1024)}, /*index=5*/f32[768]{0:T(1024)}, f32[768]...) all-reduce(f32[768]{0:T(1024)S(1)} %get-tuple-element.24, ...), channel_id=1, replica_groups=mesh['batch'=8,'grp'=4] {'batch','grp'}, use_global_device_ids=true, to_apply=%region_23.24 | all-reduce | flops 11776 | bytes 94208 | tf_op jit(solution)/shard_map/psum | solution.py:300
  393.7 3.9 gather_fusion.1
  397.5 3.4 gather_fusion
  400.9 3.4 gather_fusion.2
  404.3 110.0 %reduce-scatter.6.cloned.1.call-done = f32[1,96,576]{2,1,0:T(8,128)} async-done(((f32[32,96,576]{2,1,0:T(8,128)}), f32[1,96,576]{2,1,0:T(8,128)}) %reduce-scatter.6.cloned.1.call-update) | async-done | bytes 221200 | tf_op jit(solution)/shard_map/reduce_scatter | solution.py:318
  514.3 142.3 %reduce-scatter.10.cloned.1.call-done = f32[1,96,768]{2,1,0:T(8,128)} async-done(((f32[32,96,768]{2,1,0:T(8,128)}), f32[1,96,768]{2,1,0:T(8,128)}) %reduce-scatter.10.cloned.1.call-update) | async-done | bytes 294928 | tf_op jit(solution)/shard_map/reduce_scatter | solution.py:330
  656.6 141.0 %reduce-scatter.12.cloned.1.call-done = f32[1,384,192]{1,2,0:T(8,128)} async-done(((f32[32,384,192]{1,2,0:T(8,128)}), f32[1,384,192]{1,2,0:T(8,128)}) %reduce-scatter.12.cloned.1.call-update) | async-done | bytes 294928 | tf_op jit(solution)/shard_map/reduce_scatter | solution.py:336
  (212 shorter events, 47.9 us)
Async XLA Ops:
  7.2 82.1 %copy-start = (bf16[768,2304]{1,0:T(8,128)(2,1)S(1)}, bf16[768,2304]{1,0:T(8,128)(2,1)}, u32[]{:S(2)}) copy-start(bf16[768,2304]{1,0:T(8,128)(2,1)} %param.29) | copy-start | bytes 10616836
  10.3 47.0 %copy-start.47 = (s32[256,1]{0,1:T(1,128)}, s32[256,1]{0,1:T(1,128)S(1)}, u32[]{:S(2)}) copy-start(s32[256,1]{0,1:T(1,128)S(1)} %compare_select_fusion) | copy-start | bytes 3076
  13.2 13.7 %all-to-all-start.1 = ((bf16[8,1,64]{2,1,0:T(2,128)(2,1)}), bf16[8,1,64]{2,1,0:T(2,128)(2,1)S(1)}, u32[]{:S(2)}, u32[]{:S(2)}) async-start(bf16[8,1,64]{2,1,0:T(2,128)(2,1)} %all_to_all.28), calls=%async_computation.1 | async-start | bytes 8192 | tf_op jit(solution)/shard_map/all_to_all | solution.py:130
  20.5 38.4 %copy-start.43 = (s32[1,512]{1,0:T(1,128)S(1)}, s32[1,512]{1,0:T(1,128)}, u32[]{:S(2)}) copy-start(s32[1,512]{1,0:T(1,128)} %param.24) | copy-start | bytes 6148
  26.8 53.4 %all-to-all-start = ((bf16[8,64,768]{2,1,0:T(8,128)(2,1)}), bf16[8,64,768]{2,1,0:T(8,128)(2,1)}, u32[]{:S(2)}, u32[]{:S(2)}) async-start(bf16[8,64,768]{2,1,0:T(8,128)(2,1)} %bitcast.206), calls=%async_computation | async-start | bytes 1572864 | tf_op jit(solution)/shard_map/all_to_all | solution.py:127
  35.7 19.8 %collective-permute-start = (bf16[1,1,64,768]{3,2,0,1:T(8,128)(2,1)}, bf16[1,1,64,768]{3,2,0,1:T(8,128)(2,1)}, u32[]{:S(2)}, u32[]{:S(2)}) collective-permute-start(bf16[1,1,64,768]{3,2,0,1:T(8,128)(2,1)} %constant_dynamic-slice_fusion.6), channel_id=1, source_target_pairs={{0,4},{4,8},{8,12},{12,16},{16,20},{20,24},{24,28},{28,0},{1,5},{5... | collective-permute-start | bytes 294920 | tf_op jit(solution)/shard_map/ppermute | solution.py:122
  38.2 49.6 %copy-start.22 = (f32[768]{0:T(1024)}, f32[768]{0:T(1024)S(1)}, u32[]{:S(2)}) copy-start(f32[768]{0:T(1024)S(1)} %convert_element_type.142) | copy-start | bytes 9220
  57.4 9.2 %collective-permute-start.1 = (bf16[1,1,64,768]{3,2,0,1:T(8,128)(2,1)S(1)}, bf16[1,1,64,768]{3,2,0,1:T(8,128)(2,1)S(1)}, u32[]{:S(2)}, u32[]{:S(2)}) collective-permute-start(bf16[1,1,64,768]{3,2,0,1:T(8,128)(2,1)S(1)} %get-tuple-element.65), channel_id=1, source_target_pairs={{0,8},{4,12},{8,16},{12,20},{16,24},{20,28},{24,0},{28,4},{1,9},{5... | collective-permute-start | bytes 294920 | tf_op jit(solution)/shard_map/ppermute | solution.py:122
  59.8 19.7 %collective-permute-start.6 = (bf16[1,1,64,768]{3,2,0,1:T(8,128)(2,1)S(1)}, bf16[1,1,64,768]{3,2,0,1:T(8,128)(2,1)S(1)}, u32[]{:S(2)}, u32[]{:S(2)}) collective-permute-start(bf16[1,1,64,768]{3,2,0,1:T(8,128)(2,1)S(1)} %get-tuple-element.60), channel_id=1, source_target_pairs={{0,28},{4,0},{8,4},{12,8},{16,12},{20,16},{24,20},{28,24},{1,29},{... | collective-permute-start | bytes 294920 | tf_op jit(solution)/shard_map/ppermute | solution.py:122
  63.1 15.8 %collective-permute-start.5 = (bf16[1,1,64,768]{3,2,0,1:T(8,128)(2,1)S(1)}, bf16[1,1,64,768]{3,2,0,1:T(8,128)(2,1)S(1)}, u32[]{:S(2)}, u32[]{:S(2)}) collective-permute-start(bf16[1,1,64,768]{3,2,0,1:T(8,128)(2,1)S(1)} %get-tuple-element.61), channel_id=1, source_target_pairs={{0,24},{4,28},{8,0},{12,4},{16,8},{20,12},{24,16},{28,20},{1,25},{... | collective-permute-start | bytes 294920 | tf_op jit(solution)/shard_map/ppermute | solution.py:122
  63.2 15.0 %collective-permute-start.4 = (bf16[1,1,64,768]{3,2,0,1:T(8,128)(2,1)S(1)}, bf16[1,1,64,768]{3,2,0,1:T(8,128)(2,1)S(1)}, u32[]{:S(2)}, u32[]{:S(2)}) collective-permute-start(bf16[1,1,64,768]{3,2,0,1:T(8,128)(2,1)S(1)} %get-tuple-element.62), channel_id=1, source_target_pairs={{0,20},{4,24},{8,28},{12,0},{16,4},{20,8},{24,12},{28,16},{1,21},{... | collective-permute-start | bytes 294920 | tf_op jit(solution)/shard_map/ppermute | solution.py:122
  64.2 13.4 %collective-permute-start.3 = (bf16[1,1,64,768]{3,2,0,1:T(8,128)(2,1)S(1)}, bf16[1,1,64,768]{3,2,0,1:T(8,128)(2,1)S(1)}, u32[]{:S(2)}, u32[]{:S(2)}) collective-permute-start(bf16[1,1,64,768]{3,2,0,1:T(8,128)(2,1)S(1)} %get-tuple-element.63), channel_id=1, source_target_pairs={{0,16},{4,20},{8,24},{12,28},{16,0},{20,4},{24,8},{28,12},{1,17},{... | collective-permute-start | bytes 294920 | tf_op jit(solution)/shard_map/ppermute | solution.py:122
  66.5 10.4 %collective-permute-start.2 = (bf16[1,1,64,768]{3,2,0,1:T(8,128)(2,1)S(1)}, bf16[1,1,64,768]{3,2,0,1:T(8,128)(2,1)S(1)}, u32[]{:S(2)}, u32[]{:S(2)}) collective-permute-start(bf16[1,1,64,768]{3,2,0,1:T(8,128)(2,1)S(1)} %get-tuple-element.64), channel_id=1, source_target_pairs={{0,12},{4,16},{8,20},{12,24},{16,28},{20,0},{24,4},{28,8},{1,13},{... | collective-permute-start | bytes 294920 | tf_op jit(solution)/shard_map/ppermute | solution.py:122
  80.2 61.5 %all-to-all-start.4 = ((bf16[8,64,1024]{2,1,0:T(8,128)(2,1)}), bf16[8,64,1024]{2,1,0:T(8,128)(2,1)}, u32[]{:S(2)}, u32[]{:S(2)}) async-start(bf16[8,64,1024]{2,1,0:T(8,128)(2,1)} %bitcast.195), calls=%async_computation.4 | async-start | bytes 2097152 | tf_op jit(solution)/shard_map/all_to_all | solution.py:129
  84.5 319.8 %reduce-scatter.8.cloned.1.call-start = ((), (), s32[]{:S(2)}) async-start(), calls=%async_computation.12 | async-start | bytes 3244032 | tf_op jit(solution)/shard_map/reduce_scatter | solution.py:324
  86.2 5.2 copy-start.24
  87.8 3.6 copy-start.28
  87.8 3.6 copy-start.26
  89.3 3.1 copy-start.35
  89.4 3.1 copy-start.36
  104.4 4.6 copy-start.1
  104.4 4.7 copy-start.19
  108.1 6.3 copy-start.21
  109.1 5.3 copy-start.50
  109.1 5.3 copy-start.51
  114.4 2.8 copy-start.16
  114.5 22.4 %slice-start.3 = ((s8[4718592]{0:T(1024)(128)(4,1)}), s8[4194304]{0:T(1024)(128)(4,1)S(1)}, s32[]{:S(2)}) async-start(s8[4718592]{0:T(1024)(128)(4,1)} %bitcast.224), calls=%async_computation.19 | async-start | bytes 8388608
  116.8 20.0 %copy-start.9 = (f32[512,768]{1,0:T(8,128)}, f32[512,768]{1,0:T(8,128)S(1)}, u32[]{:S(2)}) copy-start(f32[512,768]{1,0:T(8,128)S(1)} %get-tuple-element.70) | copy-start | bytes 4718596
  117.2 19.7 %copy-start.45 = (f32[512]{0:T(512)}, f32[512]{0:T(512)S(1)}, u32[]{:S(2)}) copy-start(f32[512]{0:T(512)S(1)} %fusion.43) | copy-start | bytes 6148
  117.2 19.7 %copy-start.49 = (f32[768]{0:T(1024)S(1)}, f32[768]{0:T(1024)}, u32[]{:S(2)}) copy-start(f32[768]{0:T(1024)} %convert_element_type.159) | copy-start | bytes 9220
  117.2 19.7 %slice-start.4 = ((s8[4718592]{0:T(1024)(128)(4,1)}), s8[524288]{0:T(1024)(128)(4,1)S(1)}, s32[]{:S(2)}) async-start(s8[4718592]{0:T(1024)(128)(4,1)} %bitcast.224), calls=%async_computation.20 | async-start | bytes 1048576
  141.7 4.3 copy-start.8
  141.7 4.3 copy-start.31
  141.7 4.3 copy-start.33
  141.7 4.3 copy-start.44
  141.7 6.7 slice-start.5
  146.1 12.6 %slice-start.7 = ((s8[4718592]{0:T(1024)(128)(4,1)}), s8[4194304]{0:T(1024)(128)(4,1)S(1)}, s32[]{:S(2)}) async-start(s8[4718592]{0:T(1024)(128)(4,1)} %bitcast.228), calls=%async_computation.23 | async-start | bytes 8388608
  148.4 10.3 %copy-start.18 = (bf16[512,768]{1,0:T(8,128)(2,1)}, bf16[512,768]{1,0:T(8,128)(2,1)S(1)}, u32[]{:S(2)}) copy-start(bf16[512,768]{1,0:T(8,128)(2,1)S(1)} %get-tuple-element.45) | copy-start | bytes 2359300
  149.0 9.7 %copy-start.10 = (f32[512,768]{1,0:T(8,128)S(1)}, f32[512,768]{1,0:T(8,128)}, u32[]{:S(2)}) copy-start(f32[512,768]{1,0:T(8,128)} %copy-done.9) | copy-start | bytes 4718596
  149.0 9.7 %copy-start.38 = (f32[768]{0:T(1024)S(1)}, f32[768]{0:T(1024)}, u32[]{:S(2)}) copy-start(f32[768]{0:T(1024)} %convert_element_type.154) | copy-start | bytes 9220
  149.0 9.7 %copy-start.46 = (f32[512]{0:T(512)S(1)}, f32[512]{0:T(512)}, u32[]{:S(2)}) copy-start(f32[512]{0:T(512)} %copy-done.45) | copy-start | bytes 6148
  149.0 9.7 %slice-start.8 = ((s8[4718592]{0:T(1024)(128)(4,1)}), s8[524288]{0:T(1024)(128)(4,1)S(1)}, s32[]{:S(2)}) async-start(s8[4718592]{0:T(1024)(128)(4,1)} %bitcast.228), calls=%async_computation.24 | async-start | bytes 1048576
  173.1 231.2 %reduce-scatter.14.cloned.1.call-start = ((), (), s32[]{:S(2)}) async-start(), calls=%async_computation.15 | async-start | bytes 3244032 | tf_op jit(solution)/shard_map/reduce_scatter | solution.py:342
  191.5 322.8 %reduce-scatter.6.cloned.1.call-start = ((), (), s32[]{:S(2)}) async-start(), calls=%async_computation.11 | async-start | bytes 8110080 | tf_op jit(solution)/shard_map/reduce_scatter | solution.py:318
  191.7 13.8 %slice-start = ((s8[12582912]{0:T(1024)(128)(4,1)}), s8[4194304]{0:T(1024)(128)(4,1)S(1)}, s32[]{:S(2)}) async-start(s8[12582912]{0:T(1024)(128)(4,1)} %bitcast.175), calls=%async_computation.16 | async-start | bytes 8388608
  191.7 13.8 %slice-start.1 = ((s8[12582912]{0:T(1024)(128)(4,1)}), s8[4194304]{0:T(1024)(128)(4,1)S(1)}, s32[]{:S(2)}) async-start(s8[12582912]{0:T(1024)(128)(4,1)} %bitcast.175), calls=%async_computation.17 | async-start | bytes 8388608
  191.8 13.8 %slice-start.2 = ((s8[12582912]{0:T(1024)(128)(4,1)}), s8[4194304]{0:T(1024)(128)(4,1)S(1)}, s32[]{:S(2)}) async-start(s8[12582912]{0:T(1024)(128)(4,1)} %bitcast.175), calls=%async_computation.18 | async-start | bytes 8388608
  191.8 13.8 %copy-start.6 = (pred[512,512]{0,1:T(8,128)(4,1)S(1)}, pred[512,512]{0,1:T(8,128)(4,1)}, u32[]{:S(2)}) copy-start(pred[512,512]{0,1:T(8,128)(4,1)} %fusion.32) | copy-start | bytes 786436
  191.8 13.8 %copy-start.20 = (f32[12,512]{1,0:T(8,128)S(1)}, f32[12,512]{1,0:T(8,128)}, u32[]{:S(2)}) copy-start(f32[12,512]{1,0:T(8,128)} %log_add_fusion) | copy-start | bytes 73732
  205.6 7.2 copy-start.3
  214.0 6.1 copy-start.4
  214.0 2.9 copy-start.12
  216.9 3.2 copy-start.15
  220.0 5.8 copy-start.13
  225.9 430.7 %reduce-scatter.10.cloned.1.call-start = ((), (), s32[]{:S(2)}) async-start(), calls=%async_computation.13 | async-start | bytes 9732096 | tf_op jit(solution)/shard_map/reduce_scatter | solution.py:330
  256.9 540.6 %reduce-scatter.12.cloned.1.call-start = ((), (), s32[]{:S(2)}) async-start(), calls=%async_computation.14 | async-start | bytes 9732096 | tf_op jit(solution)/shard_map/reduce_scatter | solution.py:336
  280.7 35.7 %copy-start.23 = (f32[768]{0:T(1024)S(1)}, f32[768]{0:T(1024)}, u32[]{:S(2)}) copy-start(f32[768]{0:T(1024)} %copy-done.22) | copy-start | bytes 9220
  280.8 35.7 %copy-start.25 = (f32[512]{0:T(512)S(1)}, f32[512]{0:T(512)}, u32[]{:S(2)}) copy-start(f32[512]{0:T(512)} %copy-done.24) | copy-start | bytes 6148
  312.2 27.4 %all-to-all-start.2 = ((bf16[8,64,768]{2,1,0:T(8,128)(2,1)}), bf16[8,64,768]{2,1,0:T(8,128)(2,1)}, u32[]{:S(2)}, u32[]{:S(2)}) async-start(bf16[8,64,768]{2,1,0:T(8,128)(2,1)} %bitcast.200), calls=%async_computation.2 | async-start | bytes 1572864 | tf_op jit(solution)/shard_map/all_to_all | solution.py:262
  316.5 4.8 copy-start.29
  316.5 4.8 copy-start.27
  326.6 22.4 %copy-start.30 = (f32[768]{0:T(1024)S(1)}, f32[768]{0:T(1024)}, u32[]{:S(2)}) copy-start(f32[768]{0:T(1024)} %get-tuple-element.57) | copy-start | bytes 9220
  339.6 61.3 %all-to-all-start.5 = ((bf16[8,64,768]{2,1,0:T(8,128)(2,1)}), bf16[8,64,768]{2,1,0:T(8,128)(2,1)}, u32[]{:S(2)}, u32[]{:S(2)}) async-start(bf16[8,64,768]{2,1,0:T(8,128)(2,1)} %bitcast.203), calls=%async_computation.5 | async-start | bytes 1572864 | tf_op jit(solution)/shard_map/all_to_all | solution.py:276
  393.7 3.9 copy-start.40
  (15 other events, 26.4 us)
Sparse Core Ops, SparseCore 0:
  173.2 102.9 reduce-scatter.7
  282.2 104.4 reduce-scatter.13
  392.9 121.4 reduce-scatter.5
  521.6 134.8 reduce-scatter.9
  662.9 134.5 reduce-scatter.11
